TPU v7x, 32 devices: a whole 2x2x4 slice. The times are simulated.
32 devices in a mesh: freq: 2 (over y), row: 4 (over z), col: 4 (over x, core).
Axes of the slice: x: 2, y: 2, z: 4, core: 2. Of those that a mesh axis runs over, the one named last changes fastest.
Arguments:
- traces: bfloat16 [4, 6144, 6144], P('freq', 'row', 'col'), parts along dimension 0, may hold values from -6 to 6
- recv_live: int32 [12288], P('freq'), parts along dimension 0, may hold values 0 or 1
- missing: int32 [8, 96], P('freq'), parts along dimension 0, may hold values from 0 to 1535, as said below
- wavelet: float32 [4], P('freq'), parts along dimension 0, may hold values from 0.5 to 1.5
Outputs:
- primaries: float32 [4, 6144, 512], P('freq', 'row', 'col'), parts along dimension 0
There are 2 independent parts, one for each index of `freq`. A program takes and returns all parts, laid end to end along the dimension named above; each array names one. Nothing has to cross between parts.
Inputs may be any that keep to these rules, and one draw needn't show every extreme that they name: `missing`: each row lists 96 distinct positions within one block of 1536 shots, the shots of that block that were not recorded; the block's first and last shots are always among them.
All inputs are finite; a program needn't handle non-finite values.
Results may differ from a plain program's by a relative error of at most 0.0003.
Values may be sent and summed in bfloat16 or wider, within the bound.
A program may use at most 128 MiB of HBM per device.

v0:
```python
import math
import jax
import jax.numpy as jnp
from jax import lax
from jax.sharding import PartitionSpec as P

ORDER = 6144
WIN = 128


def from_behind(block, axis, distance):
    devices = range(lax.axis_size(axis))
    route = [((i - distance) % len(devices), i) for i in devices]
    return lax.ppermute(block, axis, route)


def matmul(first, second):
    return jnp.dot(first, second, preferred_element_type=jnp.float32)


def complex_product(left_tile, right_tile):
    real_part = matmul(left_tile[0], right_tile[0]) - matmul(left_tile[1], right_tile[1])
    imag_part = matmul(left_tile[0], right_tile[1]) + matmul(left_tile[1], right_tile[0])
    return jnp.stack([real_part, imag_part])


def mirror(payload, grid_size, row_index, col_index):
    anti_sum = row_index + col_index
    anchors = jnp.arange(grid_size, dtype=jnp.int32)
    bit_count = grid_size.bit_length() - 1
    for bit_number in range(bit_count):
        stride = 2**bit_number
        carried = from_behind(payload, "row", stride)
        carried = from_behind(carried, "col", grid_size - stride)
        offset = (anti_sum - 2 * anchors) % grid_size
        spot_row = (anchors + offset % stride) % grid_size
        arrive = jnp.any(
            (spot_row == (row_index - stride) % grid_size) & (offset // stride % 2 == 1)
        )
        payload = jnp.where(arrive, carried, payload)
    return payload


def transpose_blocks(payload, grid_size, row_index, col_index):
    anti_sum = row_index + col_index
    anchors = jnp.arange(grid_size, dtype=jnp.int32)
    bit_count = grid_size.bit_length() - 1
    for bit_number in range(bit_count):
        stride = 2**bit_number
        carried = from_behind(payload, "row", stride)
        carried = from_behind(carried, "col", grid_size - stride)
        offset = (anti_sum - 2 * anchors) % grid_size
        spot_row = (anchors + offset % stride) % grid_size
        arrive = jnp.any(
            (spot_row == (row_index - stride) % grid_size) & (offset // stride % 2 == 1)
        )
        payload = jnp.where(arrive, carried, payload)
    return payload


def local(traces, recv_live, missing, wavelet):
    tile_size = traces.shape[1]
    grid_size = lax.axis_size("row")
    row_index = lax.axis_index("row")
    col_index = lax.axis_index("col")
    positions = jnp.arange(tile_size, dtype=jnp.int32)
    miss_row = lax.dynamic_index_in_dim(missing, row_index, 0, keepdims=False)
    miss_col = lax.dynamic_index_in_dim(missing, col_index, 0, keepdims=False)
    dead_row = jnp.any(positions[:, None] == miss_row[None, :], axis=1)
    dead_col = jnp.any(positions[:, None] == miss_col[None, :], axis=1)
    recv_row = lax.dynamic_slice_in_dim(recv_live, row_index * tile_size, tile_size) == 1
    recv_col = lax.dynamic_slice_in_dim(recv_live, col_index * tile_size, tile_size) == 1
    zero_bf = jnp.zeros((), jnp.bfloat16)
    outgoing = jnp.swapaxes(jnp.take(traces, miss_col, axis=2), 1, 2)
    incoming = mirror(outgoing, grid_size, row_index, col_index)
    direct = jnp.where(recv_col[None, None, :], traces, zero_bf)
    direct = jnp.where(dead_row[None, :, None], zero_bf, direct)
    keep_mask = jnp.take(recv_row, miss_row)[:, None] & jnp.logical_not(dead_col)[None, :]
    patched = jnp.where(keep_mask[None], incoming, zero_bf)
    filled = direct.at[:, miss_row, :].set(patched)
    window = filled[:, :, :WIN]
    win_width = window.shape[2]
    running = jnp.zeros((2, tile_size, win_width), jnp.float32)
    swapped = transpose_blocks(window, grid_size, row_index, col_index)
    gathered = lax.all_gather(swapped, "row", axis=2, tiled=True)

    def one_hop(stop_index, total):
        source_block = (col_index - stop_index - 1) % grid_size
        piece = lax.dynamic_slice_in_dim(gathered, source_block * win_width, win_width, 2)
        total = total + complex_product(filled, piece)
        return from_behind(total, "col", 1)

    running = lax.fori_loop(0, grid_size - 1, one_hop, running)
    own_piece = lax.dynamic_slice_in_dim(gathered, col_index * win_width, win_width, 2)
    running = running + complex_product(filled, own_piece)
    norm_scale = 1.0 / math.sqrt(ORDER)
    pred_real = (wavelet[0] * running[0] - wavelet[1] * running[1]) * norm_scale
    pred_imag = (wavelet[0] * running[1] + wavelet[1] * running[0]) * norm_scale
    window_f = window.astype(jnp.float32)
    return jnp.stack([window_f[0] - pred_real, window_f[1] - pred_imag])


def solution(mesh):
    in_specs = (P("freq", "row", "col"), P("freq"), P("freq", None), P("freq"))
    out_specs = P("freq", "row", "col")
    return jax.shard_map(local, mesh=mesh, in_specs=in_specs, out_specs=out_specs, check_vma=False)
```

profile of v0, /device:TPU:0, one launch (start us, length us, event | category | flops | bytes accessed | tf_op | source)
XLA Modules:
  0.0 447.0 jit_solution(11039672735321170451)
XLA Ops:
  6.5 0.8 fusion.64
  7.3 0.9 dynamic-slice_compare_fusion.1
  8.2 1.3 gather_fusion
  9.5 0.8 compare_and_fusion
  10.2 24.0 %copy.16 = bf16[2,1536,1536]{1,0,2:T(2,128)(2,1)} copy(bf16[2,1536,1536]{2,1,0:T(8,128)(2,1)} %param.6) | data formatting | bytes 18874368 | tf_op args[0]
  34.2 5.5 %gather_fusion.1 = bf16[96,2,1536]{2,1,0:T(2,128)(2,1)S(1)} fusion(bf16[2,1536,1536]{1,0,2:T(2,128)(2,1)} %copy.16, s32[1024]{0:T(1024)S(1)} %get-tuple-element.183), kind=kCustom, calls=%fused_computation.1 | custom fusion | bytes 1180032 | tf_op jit(solution)/shard_map/jit(_take)/gather | solution.py:74
  39.7 0.6 fusion.53
  40.3 3.1 collective-permute-start.1
  43.4 15.3 %collective-permute-done.1 = bf16[2,96,1536]{2,0,1:T(2,128)(2,1)S(1)} collective-permute-done((bf16[2,96,1536]{2,0,1:T(2,128)(2,1)S(1)}, bf16[2,96,1536]{2,0,1:T(2,128)(2,1)S(1)}, u32[]{:S(2)}, u32[]{:S(2)}) %collective-permute-start.1) | collective-permute-done | bytes 589856 | tf_op jit(solution)/shard_map/ppermute | solution.py:14
  58.7 0.2 collective-permute-start.2
  59.0 0.7 and_reduce_fusion
  59.6 6.7 %collective-permute-done.2 = bf16[2,96,1536]{2,0,1:T(2,128)(2,1)S(1)} collective-permute-done((bf16[2,96,1536]{2,0,1:T(2,128)(2,1)S(1)}, bf16[2,96,1536]{2,0,1:T(2,128)(2,1)S(1)}, u32[]{:S(2)}, u32[]{:S(2)}) %collective-permute-start.2) | collective-permute-done | bytes 589856 | tf_op jit(solution)/shard_map/ppermute | solution.py:14
  66.4 1.5 broadcast_select_fusion.3
  67.8 0.7 collective-permute-start.3
  68.5 0.2 fusion.54
  68.7 27.9 %collective-permute-done.3 = bf16[2,96,1536]{2,0,1:T(2,128)(2,1)S(1)} collective-permute-done((bf16[2,96,1536]{2,0,1:T(2,128)(2,1)S(1)}, bf16[2,96,1536]{2,0,1:T(2,128)(2,1)S(1)}, u32[]{:S(2)}, u32[]{:S(2)}) %collective-permute-start.3) | collective-permute-done | bytes 589856 | tf_op jit(solution)/shard_map/ppermute | solution.py:14
  96.6 1.4 collective-permute-start.4
  98.0 42.0 %broadcast_select_fusion = bf16[2,1536,1536]{2,0,1:T(2,128)(2,1)} fusion(pred[1536]{0:T(1024)(128)(4,1)S(1)} %fusion.54, pred[1536]{0:T(1024)(128)(4,1)S(1)} %get-tuple-element.175, bf16[2,1536,1536]{2,1,0:T(8,128)(2,1)} %param.6), kind=kLoop, calls=%fused_computation.26 | loop fusion | flops 9437184 | bytes 18877440 | tf_op jit(solution)/shard_map/jit(_where)/select_n | solution.py:77
  139.9 0.2 fusion.55
  140.1 0.6 and_reduce_fusion.1
  140.7 0.1 broadcast_and_fusion
  140.9 1.7 fusion.52
  142.6 11.7 %scatter_fusion = bf16[2,1536,1536]{2,0,1:T(2,128)(2,1)} fusion(bf16[2,1536,1536]{2,0,1:T(2,128)(2,1)} %broadcast_select_fusion, s32[96]{0:T(128)S(1)} %get-tuple-element.178, bf16[96,2,1536]{2,1,0:T(2,128)(2,1)S(1)} %fusion.52), kind=kCustom, calls=%fused_computation.2 | custom fusion | bytes 1769856 | tf_op jit(solution)/shard_map/scatter | solution.py:80
  154.3 8.8 %copy.17 = bf16[2,1536,1536]{2,1,0:T(8,128)(2,1)} copy(bf16[2,1536,1536]{2,0,1:T(2,128)(2,1)} %scatter_fusion) | data formatting | bytes 18874368 | tf_op jit(solution)/shard_map/scatter | solution.py:80
  163.1 1.2 slice.100
  164.4 21.1 %collective-permute-done.5 = bf16[2,1536,128]{2,1,0:T(8,128)(2,1)S(1)} collective-permute-done((bf16[2,1536,128]{2,1,0:T(8,128)(2,1)S(1)}, bf16[2,1536,128]{2,1,0:T(8,128)(2,1)S(1)}, u32[]{:S(2)}, u32[]{:S(2)}) %collective-permute-start.5) | collective-permute-done | bytes 786464 | tf_op jit(solution)/shard_map/ppermute | solution.py:14
  185.4 9.5 %collective-permute-done.6 = bf16[2,1536,128]{2,1,0:T(8,128)(2,1)S(1)} collective-permute-done((bf16[2,1536,128]{2,1,0:T(8,128)(2,1)S(1)}, bf16[2,1536,128]{2,1,0:T(8,128)(2,1)S(1)}, u32[]{:S(2)}, u32[]{:S(2)}) %collective-permute-start.6) | collective-permute-done | bytes 786464 | tf_op jit(solution)/shard_map/ppermute | solution.py:14
  194.9 3.1 broadcast_select_fusion.6
  198.0 36.1 %collective-permute-done.7 = bf16[2,1536,128]{2,1,0:T(8,128)(2,1)S(1)} collective-permute-done((bf16[2,1536,128]{2,1,0:T(8,128)(2,1)S(1)}, bf16[2,1536,128]{2,1,0:T(8,128)(2,1)S(1)}, u32[]{:S(2)}, u32[]{:S(2)}) %collective-permute-start.7) | collective-permute-done | bytes 786464 | tf_op jit(solution)/shard_map/ppermute | solution.py:14
  234.1 0.8 collective-permute-start.8
  234.9 18.7 %collective-permute-done.8 = bf16[2,1536,128]{2,1,0:T(8,128)(2,1)S(1)} collective-permute-done((bf16[2,1536,128]{2,1,0:T(8,128)(2,1)S(1)}, bf16[2,1536,128]{2,1,0:T(8,128)(2,1)S(1)}, u32[]{:S(2)}, u32[]{:S(2)}) %collective-permute-start.8) | collective-permute-done | bytes 786464 | tf_op jit(solution)/shard_map/ppermute | solution.py:14
  253.7 1.5 broadcast_select_fusion.7
  255.2 0.6 fusion.70
  255.8 19.5 %fusion.69 = (bf16[1,1536,1536]{2,0,1:T(2,128)(2,1)}, bf16[1,1536,1536]{2,0,1:T(2,128)(2,1)}) fusion(bf16[2,1536,1536]{2,0,1:T(2,128)(2,1)} %scatter_fusion), kind=kLoop, calls=%fused_computation.104 | loop fusion | bytes 18874368 | tf_op jit(solution)/shard_map/slice | solution.py:22
  275.4 42.8 %all-gather.2.cloned.1.call-done = bf16[2,1536,512]{2,1,0:T(8,128)(2,1)} async-done(((bf16[2,1536,128]{2,1,0:T(8,128)(2,1)}), bf16[2,1536,512]{2,1,0:T(8,128)(2,1)}) %all-gather.2.cloned.1.call-update) | async-done | bytes 3145744 | tf_op jit(solution)/shard_map/all_gather | solution.py:85
  318.2 0.2 broadcast_in_dim.71
  318.3 101.8 %while.15 = (s32[]{:T(128)}, f32[2,1536,128]{1,2,0:T(8,128)S(1)}, s32[]{:T(128)}, bf16[2,1536,512]{2,1,0:T(8,128)(2,1)}, bf16[2,1536,1536]{2,1,0:T(8,128)(2,1)},...) while((s32[]{:T(128)}, f32[2,1536,128]{1,2,0:T(8,128)S(1)}, ...), condition=%wide.region_6.7_spmd, body=%wide.region_5.6_spmd.sunk | while | flops 2417098752 | bytes 73925016 | solution.py:93
  318.4 4.3 fusion.83
  322.7 4.2 fusion.85
  326.9 2.7 fusion.84
  329.5 2.7 fusion.86
  332.2 0.2 maximum_add_fusion.3
  332.5 19.8 %collective-permute-done = f32[2,1536,128]{1,2,0:T(8,128)S(1)} collective-permute-done((f32[2,1536,128]{1,2,0:T(8,128)S(1)}, f32[2,1536,128]{1,2,0:T(8,128)S(1)}, u32[]{:S(2)}, u32[]{:S(2)}) %collective-permute-start) | collective-permute-done | bytes 1572896 | tf_op jit(solution)/shard_map/while/body/eval_jaxpr/ppermute | solution.py:14
  352.3 4.3 fusion.83
  356.6 4.2 fusion.85
  360.8 2.7 fusion.84
  363.5 2.7 fusion.86
  366.1 0.2 maximum_add_fusion.3
  366.4 19.8 %collective-permute-done = f32[2,1536,128]{1,2,0:T(8,128)S(1)} collective-permute-done((f32[2,1536,128]{1,2,0:T(8,128)S(1)}, f32[2,1536,128]{1,2,0:T(8,128)S(1)}, u32[]{:S(2)}, u32[]{:S(2)}) %collective-permute-start) | collective-permute-done | bytes 1572896 | tf_op jit(solution)/shard_map/while/body/eval_jaxpr/ppermute | solution.py:14
  386.2 4.3 fusion.83
  390.5 4.2 fusion.85
  394.7 2.7 fusion.84
  397.4 2.7 fusion.86
  400.1 0.2 maximum_add_fusion.3
  400.3 19.8 %collective-permute-done = f32[2,1536,128]{1,2,0:T(8,128)S(1)} collective-permute-done((f32[2,1536,128]{1,2,0:T(8,128)S(1)}, f32[2,1536,128]{1,2,0:T(8,128)S(1)}, u32[]{:S(2)}, u32[]{:S(2)}) %collective-permute-start) | collective-permute-done | bytes 1572896 | tf_op jit(solution)/shard_map/while/body/eval_jaxpr/ppermute | solution.py:14
  420.2 0.5 copy.19
  420.6 5.3 %fusion.28 = f32[1536,128]{1,0:T(8,128)S(1)} fusion(bf16[1,1536,1536]{2,0,1:T(2,128)(2,1)} %get-tuple-element.170, bf16[2,1536,512]{2,1,0:T(8,128)(2,1)} %get-tuple-element.269, s32[]{:T(128)S(6)} %select_n.231), kind=kOutput, calls=%fused_computation.28 | convolution fusion | flops 603979776 | bytes 10616836 | tf_op jit(solution)/shard_map/dot_general | solution.py:18
  425.9 5.2 %fusion.30 = f32[1536,128]{1,0:T(8,128)S(1)} fusion(bf16[1,1536,1536]{2,0,1:T(2,128)(2,1)} %get-tuple-element.170, bf16[2,1536,512]{2,1,0:T(8,128)(2,1)} %get-tuple-element.269, s32[]{:T(128)S(6)} %add.229, s32[]{:T(128)S(6)} %select_n.231), kind=kOutput, calls=%fused_computation.30 | convolution fusion | flops 603979776 | bytes 10616840 | tf_op jit(solution)/shard_map/dot_general | solution.py:18
  431.2 2.4 fusion.42
  433.6 2.4 fusion.45
  436.0 0.2 maximum_add_fusion.1
  436.2 1.2 copy-done.1
  437.4 1.5 slice_subtract_fusion.1
  438.9 1.2 pad_maximum_fusion
  (27 shorter events, 0.3 us)
Async XLA Ops:
  6.5 311.6 %all-gather.2.cloned.1.call-start = ((), (), s32[]{:S(2)}) async-start(), calls=%async_computation | async-start | bytes 3932160 | tf_op jit(solution)/shard_map/all_gather | solution.py:85
  40.3 18.4 %collective-permute-start.1 = (bf16[2,96,1536]{2,0,1:T(2,128)(2,1)S(1)}, bf16[2,96,1536]{2,0,1:T(2,128)(2,1)S(1)}, u32[]{:S(2)}, u32[]{:S(2)}) collective-permute-start(bf16[2,96,1536]{2,0,1:T(2,128)(2,1)S(1)} %fusion.53), channel_id=1, source_target_pairs={{12,0},{0,4},{4,8},{8,12},{13,1},{1,5},{5,9},{9,13},{14,2},{2,6},{... | collective-permute-start | bytes 1769480 | tf_op jit(solution)/shard_map/ppermute | solution.py:14
  58.7 7.6 %collective-permute-start.2 = (bf16[2,96,1536]{2,0,1:T(2,128)(2,1)S(1)}, bf16[2,96,1536]{2,0,1:T(2,128)(2,1)S(1)}, u32[]{:S(2)}, u32[]{:S(2)}) collective-permute-start(bf16[2,96,1536]{2,0,1:T(2,128)(2,1)S(1)} %collective-permute-done.1), channel_id=1, source_target_pairs={{1,0},{2,1},{3,2},{0,3},{5,4},{6,5},{7,6},{4,7},{9,8},{10,9},{11,1... | collective-permute-start | bytes 1769480 | tf_op jit(solution)/shard_map/ppermute | solution.py:14
  67.8 28.7 %collective-permute-start.3 = (bf16[2,96,1536]{2,0,1:T(2,128)(2,1)S(1)}, bf16[2,96,1536]{2,0,1:T(2,128)(2,1)S(1)}, u32[]{:S(2)}, u32[]{:S(2)}) collective-permute-start(bf16[2,96,1536]{2,0,1:T(2,128)(2,1)S(1)} %broadcast_select_fusion.3), channel_id=1, source_target_pairs={{8,0},{12,4},{0,8},{4,12},{9,1},{13,5},{1,9},{5,13},{10,2},{14,6},... | collective-permute-start | bytes 1769480 | tf_op jit(solution)/shard_map/ppermute | solution.py:14
  96.6 44.3 %collective-permute-start.4 = (bf16[2,96,1536]{2,0,1:T(2,128)(2,1)S(1)}, bf16[2,96,1536]{2,0,1:T(2,128)(2,1)S(1)}, u32[]{:S(2)}, u32[]{:S(2)}) collective-permute-start(bf16[2,96,1536]{2,0,1:T(2,128)(2,1)S(1)} %collective-permute-done.3), channel_id=1, source_target_pairs={{2,0},{3,1},{0,2},{1,3},{6,4},{7,5},{4,6},{5,7},{10,8},{11,9},{8,1... | collective-permute-start | bytes 1769480 | tf_op jit(solution)/shard_map/ppermute | solution.py:14
  163.1 92.1 %copy-start.2 = (f32[2]{0:T(128)S(1)}, f32[2]{0:T(128)}, u32[]{:S(2)}) copy-start(f32[2]{0:T(128)} %param.9) | copy-start | bytes 28
  164.3 21.1 %collective-permute-start.5 = (bf16[2,1536,128]{2,1,0:T(8,128)(2,1)S(1)}, bf16[2,1536,128]{2,1,0:T(8,128)(2,1)S(1)}, u32[]{:S(2)}, u32[]{:S(2)}) collective-permute-start(bf16[2,1536,128]{2,1,0:T(8,128)(2,1)S(1)} %slice.100), channel_id=1, source_target_pairs={{12,0},{0,4},{4,8},{8,12},{13,1},{1,5},{5,9},{9,13},{14,2},{2,6},{... | collective-permute-start | bytes 2359304 | tf_op jit(solution)/shard_map/ppermute | solution.py:14
  185.4 9.5 %collective-permute-start.6 = (bf16[2,1536,128]{2,1,0:T(8,128)(2,1)S(1)}, bf16[2,1536,128]{2,1,0:T(8,128)(2,1)S(1)}, u32[]{:S(2)}, u32[]{:S(2)}) collective-permute-start(bf16[2,1536,128]{2,1,0:T(8,128)(2,1)S(1)} %collective-permute-done.5), channel_id=1, source_target_pairs={{1,0},{2,1},{3,2},{0,3},{5,4},{6,5},{7,6},{4,7},{9,8},{10,9},{11,1... | collective-permute-start | bytes 2359304 | tf_op jit(solution)/shard_map/ppermute | solution.py:14
  198.0 36.1 %collective-permute-start.7 = (bf16[2,1536,128]{2,1,0:T(8,128)(2,1)S(1)}, bf16[2,1536,128]{2,1,0:T(8,128)(2,1)S(1)}, u32[]{:S(2)}, u32[]{:S(2)}) collective-permute-start(bf16[2,1536,128]{2,1,0:T(8,128)(2,1)S(1)} %get-tuple-element.171), channel_id=1, source_target_pairs={{8,0},{12,4},{0,8},{4,12},{9,1},{13,5},{1,9},{5,13},{10,2},{14,6},... | collective-permute-start | bytes 2359304 | tf_op jit(solution)/shard_map/ppermute | solution.py:14
  234.1 19.6 %collective-permute-start.8 = (bf16[2,1536,128]{2,1,0:T(8,128)(2,1)S(1)}, bf16[2,1536,128]{2,1,0:T(8,128)(2,1)S(1)}, u32[]{:S(2)}, u32[]{:S(2)}) collective-permute-start(bf16[2,1536,128]{2,1,0:T(8,128)(2,1)S(1)} %collective-permute-done.7), channel_id=1, source_target_pairs={{2,0},{3,1},{0,2},{1,3},{6,4},{7,5},{4,6},{5,7},{10,8},{11,9},{8,1... | collective-permute-start | bytes 2359304 | tf_op jit(solution)/shard_map/ppermute | solution.py:14
  318.4 8.5 %copy-start = (bf16[2,1536,1536]{2,1,0:T(8,128)(2,1)S(1)}, bf16[2,1536,1536]{2,1,0:T(8,128)(2,1)}, u32[]{:S(2)}) copy-start(bf16[2,1536,1536]{2,1,0:T(8,128)(2,1)} %get-tuple-element.246) | copy-start | bytes 28311556 | tf_op jit(solution)/shard_map/while
  332.4 19.9 %collective-permute-start = (f32[2,1536,128]{1,2,0:T(8,128)S(1)}, f32[2,1536,128]{1,2,0:T(8,128)S(1)}, u32[]{:S(2)}, u32[]{:S(2)}) collective-permute-start(f32[2,1536,128]{1,2,0:T(8,128)S(1)} %maximum_add_fusion.3), channel_id=1, source_target_pairs={{3,0},{0,1},{1,2},{2,3},{7,4},{4,5},{5,6},{6,7},{11,8},{8,9},{9,10... | collective-permute-start | bytes 4718600 | tf_op jit(solution)/shard_map/while/body/eval_jaxpr/ppermute | solution.py:14
  352.3 8.5 %copy-start = (bf16[2,1536,1536]{2,1,0:T(8,128)(2,1)S(1)}, bf16[2,1536,1536]{2,1,0:T(8,128)(2,1)}, u32[]{:S(2)}) copy-start(bf16[2,1536,1536]{2,1,0:T(8,128)(2,1)} %get-tuple-element.246) | copy-start | bytes 28311556 | tf_op jit(solution)/shard_map/while
  366.3 19.9 %collective-permute-start = (f32[2,1536,128]{1,2,0:T(8,128)S(1)}, f32[2,1536,128]{1,2,0:T(8,128)S(1)}, u32[]{:S(2)}, u32[]{:S(2)}) collective-permute-start(f32[2,1536,128]{1,2,0:T(8,128)S(1)} %maximum_add_fusion.3), channel_id=1, source_target_pairs={{3,0},{0,1},{1,2},{2,3},{7,4},{4,5},{5,6},{6,7},{11,8},{8,9},{9,10... | collective-permute-start | bytes 4718600 | tf_op jit(solution)/shard_map/while/body/eval_jaxpr/ppermute | solution.py:14
  386.2 8.5 %copy-start = (bf16[2,1536,1536]{2,1,0:T(8,128)(2,1)S(1)}, bf16[2,1536,1536]{2,1,0:T(8,128)(2,1)}, u32[]{:S(2)}) copy-start(bf16[2,1536,1536]{2,1,0:T(8,128)(2,1)} %get-tuple-element.246) | copy-start | bytes 28311556 | tf_op jit(solution)/shard_map/while
  400.3 19.9 %collective-permute-start = (f32[2,1536,128]{1,2,0:T(8,128)S(1)}, f32[2,1536,128]{1,2,0:T(8,128)S(1)}, u32[]{:S(2)}, u32[]{:S(2)}) collective-permute-start(f32[2,1536,128]{1,2,0:T(8,128)S(1)} %maximum_add_fusion.3), channel_id=1, source_target_pairs={{3,0},{0,1},{1,2},{2,3},{7,4},{4,5},{5,6},{6,7},{11,8},{8,9},{9,10... | collective-permute-start | bytes 4718600 | tf_op jit(solution)/shard_map/while/body/eval_jaxpr/ppermute | solution.py:14
  420.6 10.5 %slice-start = ((s8[9437184]{0:T(1024)(128)(4,1)}), s8[4194304]{0:T(1024)(128)(4,1)S(1)}, s32[]{:S(2)}) async-start(s8[9437184]{0:T(1024)(128)(4,1)} %bitcast.106), calls=%async_computation.1 | async-start | bytes 8388608
  420.6 10.5 %slice-start.1 = ((s8[9437184]{0:T(1024)(128)(4,1)}), s8[4194304]{0:T(1024)(128)(4,1)S(1)}, s32[]{:S(2)}) async-start(s8[9437184]{0:T(1024)(128)(4,1)} %bitcast.106), calls=%async_computation.2 | async-start | bytes 8388608
  425.9 5.3 %slice-start.2 = ((s8[9437184]{0:T(1024)(128)(4,1)}), s8[1048576]{0:T(1024)(128)(4,1)S(1)}, s32[]{:S(2)}) async-start(s8[9437184]{0:T(1024)(128)(4,1)} %bitcast.106), calls=%async_computation.3 | async-start | bytes 2097152
  436.0 1.4 copy-start.1
Sparse Core Ops, SparseCore 0:
  255.3 62.7 all-gather.1
where the time goes:
time: 449 us; the launch traced here: 447 us
  waiting for transfers between devices  238 us (53%)
  local copies, waits for them, and re-layouts  74.4 us (17%)
  other arithmetic  58 us (13%)
  matrix products  56.7 us (13%)
  between operations  13.6 us (3%)
  starting transfers between devices  6.5 us (1%)
    ppermute x11, waiting for transfers between devices, from_behind(): return lax.ppermute(block, axis, route)  195 us
    dot_general x16, matrix products, matmul(): return jnp.dot(first, second, preferred_element_type=jnp.float32)  56.7 us
    all_gather x1, waiting for transfers between devices, local(): gathered = lax.all_gather(swapped, 'row', axis=2, tiled=True)  42.8 us
    select_n x1, other arithmetic, local(): direct = jnp.where(dead_row[None, :, None], zero_bf, direct)  42 us
    unnamed x11, local copies, waits for them, and re-layouts  25.3 us
    scatter x2, local copies, waits for them, and re-layouts, local(): filled = direct.at[:, miss_row, :].set(patched)  20.5 us
    slice x1, local copies, waits for them, and re-layouts, complex_product(): left_tile[0]  19.5 us
  transfers between devices with their start and end apart: 12, of which 11 were waited for; matrix products, arithmetic and copies ran while one was open for 14% of the time, Pallas kernels for 0%

commit v1 on v0

--- a/solution.py
+++ b/solution.py
@@ -6,6 +6,27 @@
 
 ORDER = 6144
 WIN = 128
+
+
+def collect(x, axis, dim):
+    size, mine, rows = (lax.axis_size(axis), lax.axis_index(axis), x.shape[dim])
+    right = [(i, (i + 1) % size) for i in range(size)]
+    behind = [(i, (i - 1) % size) for i in range(size)]
+    whole = jnp.zeros((*x.shape[:dim], size * rows, *x.shape[dim + 1 :]), x.dtype)
+    whole = lax.dynamic_update_slice_in_dim(whole, x, mine * rows, axis=dim)
+    from_left = from_right = x
+    half = size // 2
+    for step in range(1, half + 1):
+        from_left = lax.ppermute(from_left, axis, right)
+        whole = lax.dynamic_update_slice_in_dim(
+            whole, from_left, (mine - step) % size * rows, axis=dim
+        )
+        if step < size - half:
+            from_right = lax.ppermute(from_right, axis, behind)
+            whole = lax.dynamic_update_slice_in_dim(
+                whole, from_right, (mine + step) % size * rows, axis=dim
+            )
+    return whole
 
 
 def from_behind(block, axis, distance):
@@ -82,7 +103,7 @@
     win_width = window.shape[2]
     running = jnp.zeros((2, tile_size, win_width), jnp.float32)
     swapped = transpose_blocks(window, grid_size, row_index, col_index)
-    gathered = lax.all_gather(swapped, "row", axis=2, tiled=True)
+    gathered = collect(swapped, "row", 2)
 
     def one_hop(stop_index, total):
         source_block = (col_index - stop_index - 1) % grid_size

time: 449 us -> 431 us (0.960)
  waiting for transfers between devices: 238 us -> 223 us
  between operations: 13.6 us -> 0.22 us
  local copies, waits for them, and re-layouts: 74.4 us -> 79.4 us
    all_gather x1 -> x0, waiting for transfers between devices: 42.8 us -> none  [local(): gathered = lax.all_gather(swapped, 'row', axis=2, tiled=True)]
    ppermute x0 -> x3, waiting for transfers between devices: none -> 28.3 us  [the longest x2 28.3 us: collect(): from_left = lax.ppermute(from_left, axis, right)]
  transfers between devices with their start and end apart: 12 -> 14, of which waited for: 11 -> 12; matrix products, arithmetic and copies ran while one was open for 14% -> 15% of each run, Pallas kernels for 0% -> 0%
where the time goes in v1:
time: 431 us; the launch traced here: 428 us
  waiting for transfers between devices  223 us (52%)
  local copies, waits for them, and re-layouts  79.4 us (18%)
  other arithmetic  57.8 us (13%)
  matrix products  56.7 us (13%)
  starting transfers between devices  10.3 us (2%)
    ppermute x11, waiting for transfers between devices, from_behind(): return lax.ppermute(block, axis, route)  195 us
    dot_general x16, matrix products, matmul(): return jnp.dot(first, second, preferred_element_type=jnp.float32)  56.7 us
    select_n x1, other arithmetic, local(): direct = jnp.where(dead_row[None, :, None], zero_bf, direct)  41.9 us
    ppermute x2, waiting for transfers between devices, collect(): from_left = lax.ppermute(from_left, axis, right)  28.3 us
    unnamed x11, local copies, waits for them, and re-layouts  25.3 us
    scatter x2, local copies, waits for them, and re-layouts, local(): filled = direct.at[:, miss_row, :].set(patched)  20.5 us
    slice x1, local copies, waits for them, and re-layouts, complex_product(): left_tile[0]  19.6 us
  transfers between devices with their start and end apart: 14, of which 12 were waited for; matrix products, arithmetic and copies ran while one was open for 15% of the time, Pallas kernels for 0%

profile of v1, /device:TPU:0, one launch (start us, length us, event | category | flops | bytes accessed | tf_op | source)
XLA Modules:
  0.0 427.7 jit_solution(6678425155860232537)
XLA Ops:
  0.0 0.8 fusion.64
  0.8 0.9 dynamic-slice_compare_fusion.1
  1.6 1.3 gather_fusion
  2.9 0.8 compare_and_fusion
  3.7 24.1 %copy.16 = bf16[2,1536,1536]{1,0,2:T(2,128)(2,1)} copy(bf16[2,1536,1536]{2,1,0:T(8,128)(2,1)} %param.6) | data formatting | bytes 18874368 | tf_op args[0]
  27.8 5.5 %gather_fusion.1 = bf16[96,2,1536]{2,1,0:T(2,128)(2,1)S(1)} fusion(bf16[2,1536,1536]{1,0,2:T(2,128)(2,1)} %copy.16, s32[1024]{0:T(1024)S(1)} %get-tuple-element.185), kind=kCustom, calls=%fused_computation.1 | custom fusion | bytes 1180032 | tf_op jit(solution)/shard_map/jit(_take)/gather | solution.py:95
  33.3 0.6 fusion.53
  33.9 3.1 collective-permute-start.1
  37.0 15.3 %collective-permute-done.1 = bf16[2,96,1536]{2,0,1:T(2,128)(2,1)S(1)} collective-permute-done((bf16[2,96,1536]{2,0,1:T(2,128)(2,1)S(1)}, bf16[2,96,1536]{2,0,1:T(2,128)(2,1)S(1)}, u32[]{:S(2)}, u32[]{:S(2)}) %collective-permute-start.1) | collective-permute-done | bytes 589856 | tf_op jit(solution)/shard_map/ppermute | solution.py:35
  52.3 0.2 collective-permute-start.2
  52.5 0.6 and_reduce_fusion
  53.1 6.8 %collective-permute-done.2 = bf16[2,96,1536]{2,0,1:T(2,128)(2,1)S(1)} collective-permute-done((bf16[2,96,1536]{2,0,1:T(2,128)(2,1)S(1)}, bf16[2,96,1536]{2,0,1:T(2,128)(2,1)S(1)}, u32[]{:S(2)}, u32[]{:S(2)}) %collective-permute-start.2) | collective-permute-done | bytes 589856 | tf_op jit(solution)/shard_map/ppermute | solution.py:35
  59.9 1.4 broadcast_select_fusion.3
  61.3 0.7 collective-permute-start.3
  62.2 27.9 %collective-permute-done.3 = bf16[2,96,1536]{2,0,1:T(2,128)(2,1)S(1)} collective-permute-done((bf16[2,96,1536]{2,0,1:T(2,128)(2,1)S(1)}, bf16[2,96,1536]{2,0,1:T(2,128)(2,1)S(1)}, u32[]{:S(2)}, u32[]{:S(2)}) %collective-permute-start.3) | collective-permute-done | bytes 589856 | tf_op jit(solution)/shard_map/ppermute | solution.py:35
  90.0 1.4 collective-permute-start.4
  91.4 41.9 %broadcast_select_fusion = bf16[2,1536,1536]{2,0,1:T(2,128)(2,1)} fusion(pred[1536]{0:T(1024)(128)(4,1)S(1)} %fusion.54, pred[1536]{0:T(1024)(128)(4,1)S(1)} %get-tuple-element.177, bf16[2,1536,1536]{2,1,0:T(8,128)(2,1)} %param.6), kind=kLoop, calls=%fused_computation.26 | loop fusion | flops 9437184 | bytes 18877440 | tf_op jit(solution)/shard_map/jit(_where)/select_n | solution.py:98
  133.6 0.6 and_reduce_fusion.1
  134.4 1.7 fusion.52
  136.1 11.7 %scatter_fusion = bf16[2,1536,1536]{2,0,1:T(2,128)(2,1)} fusion(bf16[2,1536,1536]{2,0,1:T(2,128)(2,1)} %broadcast_select_fusion, s32[96]{0:T(128)S(1)} %get-tuple-element.180, bf16[96,2,1536]{2,1,0:T(2,128)(2,1)S(1)} %fusion.52), kind=kCustom, calls=%fused_computation.2 | custom fusion | bytes 1769856 | tf_op jit(solution)/shard_map/scatter | solution.py:101
  147.7 8.8 %copy.17 = bf16[2,1536,1536]{2,1,0:T(8,128)(2,1)} copy(bf16[2,1536,1536]{2,0,1:T(2,128)(2,1)} %scatter_fusion) | data formatting | bytes 18874368 | tf_op jit(solution)/shard_map/scatter | solution.py:101
  156.5 1.2 slice.100
  157.8 21.1 %collective-permute-done.5 = bf16[2,1536,128]{2,1,0:T(8,128)(2,1)S(1)} collective-permute-done((bf16[2,1536,128]{2,1,0:T(8,128)(2,1)S(1)}, bf16[2,1536,128]{2,1,0:T(8,128)(2,1)S(1)}, u32[]{:S(2)}, u32[]{:S(2)}) %collective-permute-start.5) | collective-permute-done | bytes 786464 | tf_op jit(solution)/shard_map/ppermute | solution.py:35
  178.9 9.5 %collective-permute-done.6 = bf16[2,1536,128]{2,1,0:T(8,128)(2,1)S(1)} collective-permute-done((bf16[2,1536,128]{2,1,0:T(8,128)(2,1)S(1)}, bf16[2,1536,128]{2,1,0:T(8,128)(2,1)S(1)}, u32[]{:S(2)}, u32[]{:S(2)}) %collective-permute-start.6) | collective-permute-done | bytes 786464 | tf_op jit(solution)/shard_map/ppermute | solution.py:35
  188.4 3.0 broadcast_select_fusion.6
  191.4 36.1 %collective-permute-done.7 = bf16[2,1536,128]{2,1,0:T(8,128)(2,1)S(1)} collective-permute-done((bf16[2,1536,128]{2,1,0:T(8,128)(2,1)S(1)}, bf16[2,1536,128]{2,1,0:T(8,128)(2,1)S(1)}, u32[]{:S(2)}, u32[]{:S(2)}) %collective-permute-start.7) | collective-permute-done | bytes 786464 | tf_op jit(solution)/shard_map/ppermute | solution.py:35
  227.5 0.8 collective-permute-start.8
  228.3 18.7 %collective-permute-done.8 = bf16[2,1536,128]{2,1,0:T(8,128)(2,1)S(1)} collective-permute-done((bf16[2,1536,128]{2,1,0:T(8,128)(2,1)S(1)}, bf16[2,1536,128]{2,1,0:T(8,128)(2,1)S(1)}, u32[]{:S(2)}, u32[]{:S(2)}) %collective-permute-start.8) | collective-permute-done | bytes 786464 | tf_op jit(solution)/shard_map/ppermute | solution.py:35
  247.0 1.8 broadcast_in_dim.75
  248.8 1.7 constant_dynamic-update-slice_fusion.3
  250.5 0.6 fusion.70
  251.1 3.8 collective-permute-start.10
  254.9 17.8 %collective-permute-done.9 = bf16[2,1536,128]{2,1,0:T(8,128)(2,1)S(1)} collective-permute-done((bf16[2,1536,128]{2,1,0:T(8,128)(2,1)S(1)}, bf16[2,1536,128]{2,1,0:T(8,128)(2,1)S(1)}, u32[]{:S(2)}, u32[]{:S(2)}) %collective-permute-start.9) | collective-permute-done | bytes 786464 | tf_op jit(solution)/shard_map/ppermute | solution.py:20
  272.7 19.6 %fusion.69 = (bf16[1,1536,1536]{2,0,1:T(2,128)(2,1)}, bf16[1,1536,1536]{2,0,1:T(2,128)(2,1)}) fusion(bf16[2,1536,1536]{2,0,1:T(2,128)(2,1)} %scatter_fusion), kind=kLoop, calls=%fused_computation.108 | loop fusion | bytes 18874368 | tf_op jit(solution)/shard_map/slice | solution.py:43
  292.4 1.0 constant_dynamic-update-slice_fusion.2
  293.4 1.0 constant_dynamic-update-slice_fusion.1
  294.3 10.4 %collective-permute-done.11 = bf16[2,1536,128]{2,1,0:T(8,128)(2,1)S(1)} collective-permute-done((bf16[2,1536,128]{2,1,0:T(8,128)(2,1)S(1)}, bf16[2,1536,128]{2,1,0:T(8,128)(2,1)S(1)}, u32[]{:S(2)}, u32[]{:S(2)}) %collective-permute-start.11) | collective-permute-done | bytes 786464 | tf_op jit(solution)/shard_map/ppermute | solution.py:20
  304.8 1.0 constant_dynamic-update-slice_fusion
  305.9 101.8 %while.15 = (s32[]{:T(128)}, f32[2,1536,128]{1,2,0:T(8,128)S(1)}, s32[]{:T(128)}, bf16[2,1536,512]{2,1,0:T(8,128)(2,1)}, bf16[2,1536,1536]{2,1,0:T(8,128)(2,1)},...) while((s32[]{:T(128)}, f32[2,1536,128]{1,2,0:T(8,128)S(1)}, ...), condition=%wide.region_6.7_spmd, body=%wide.region_5.6_spmd.sunk | while | flops 2417098752 | bytes 73925016 | solution.py:114
  306.0 4.3 %fusion.83 = f32[128,1536]{1,0:T(8,128)S(1)} fusion(bf16[2,1536,1536]{2,1,0:T(8,128)(2,1)} %get-tuple-element.248, bf16[2,1536,512]{2,1,0:T(8,128)(2,1)} %get-tuple-element.247, s32[]{:T(128)S(6)} %select_n.330), kind=kOutput, calls=%fused_computation.3.clone.1 | convolution fusion | flops 603979776 | bytes 5898244 | tf_op jit(solution)/shard_map/while/body/eval_jaxpr/dot_general | solution.py:39
  310.3 4.2 fusion.85
  314.4 2.7 fusion.84
  317.1 2.7 fusion.86
  319.8 0.2 maximum_add_fusion.3
  320.1 19.8 %collective-permute-done = f32[2,1536,128]{1,2,0:T(8,128)S(1)} collective-permute-done((f32[2,1536,128]{1,2,0:T(8,128)S(1)}, f32[2,1536,128]{1,2,0:T(8,128)S(1)}, u32[]{:S(2)}, u32[]{:S(2)}) %collective-permute-start) | collective-permute-done | bytes 1572896 | tf_op jit(solution)/shard_map/while/body/eval_jaxpr/ppermute | solution.py:35
  339.9 4.3 %fusion.83 = f32[128,1536]{1,0:T(8,128)S(1)} fusion(bf16[2,1536,1536]{2,1,0:T(8,128)(2,1)} %get-tuple-element.248, bf16[2,1536,512]{2,1,0:T(8,128)(2,1)} %get-tuple-element.247, s32[]{:T(128)S(6)} %select_n.330), kind=kOutput, calls=%fused_computation.3.clone.1 | convolution fusion | flops 603979776 | bytes 5898244 | tf_op jit(solution)/shard_map/while/body/eval_jaxpr/dot_general | solution.py:39
  344.2 4.2 fusion.85
  348.4 2.7 fusion.84
  351.0 2.7 fusion.86
  353.7 0.2 maximum_add_fusion.3
  354.0 19.8 %collective-permute-done = f32[2,1536,128]{1,2,0:T(8,128)S(1)} collective-permute-done((f32[2,1536,128]{1,2,0:T(8,128)S(1)}, f32[2,1536,128]{1,2,0:T(8,128)S(1)}, u32[]{:S(2)}, u32[]{:S(2)}) %collective-permute-start) | collective-permute-done | bytes 1572896 | tf_op jit(solution)/shard_map/while/body/eval_jaxpr/ppermute | solution.py:35
  373.8 4.3 %fusion.83 = f32[128,1536]{1,0:T(8,128)S(1)} fusion(bf16[2,1536,1536]{2,1,0:T(8,128)(2,1)} %get-tuple-element.248, bf16[2,1536,512]{2,1,0:T(8,128)(2,1)} %get-tuple-element.247, s32[]{:T(128)S(6)} %select_n.330), kind=kOutput, calls=%fused_computation.3.clone.1 | convolution fusion | flops 603979776 | bytes 5898244 | tf_op jit(solution)/shard_map/while/body/eval_jaxpr/dot_general | solution.py:39
  378.1 4.2 fusion.85
  382.3 2.7 fusion.84
  385.0 2.7 fusion.86
  387.9 19.8 %collective-permute-done = f32[2,1536,128]{1,2,0:T(8,128)S(1)} collective-permute-done((f32[2,1536,128]{1,2,0:T(8,128)S(1)}, f32[2,1536,128]{1,2,0:T(8,128)S(1)}, u32[]{:S(2)}, u32[]{:S(2)}) %collective-permute-start) | collective-permute-done | bytes 1572896 | tf_op jit(solution)/shard_map/while/body/eval_jaxpr/ppermute | solution.py:35
  407.7 0.5 copy.19
  408.2 5.3 %fusion.28 = f32[1536,128]{1,0:T(8,128)S(1)} fusion(bf16[1,1536,1536]{2,0,1:T(2,128)(2,1)} %get-tuple-element.172, bf16[2,1536,512]{2,1,0:T(8,128)(2,1)} %constant_dynamic-update-slice_fusion, s32[]{:T(128)S(6)} %select_n.256), kind=kOutput, calls=%fused_computation.28 | convolution fusion | flops 603979776 | bytes 10616836 | tf_op jit(solution)/shard_map/dot_general | solution.py:39
  413.5 5.2 %fusion.30 = f32[1536,128]{1,0:T(8,128)S(1)} fusion(bf16[1,1536,1536]{2,0,1:T(2,128)(2,1)} %get-tuple-element.172, bf16[2,1536,512]{2,1,0:T(8,128)(2,1)} %constant_dynamic-update-slice_fusion, s32[]{:T(128)S(6)} %add.255, s32[]{:T(128)S(6)} %select_n.256), kind=kOutput, calls=%fused_computation.30 | convolution fusion | flops 603979776 | bytes 10616840 | tf_op jit(solution)/shard_map/dot_general | solution.py:39
  418.8 2.4 fusion.42
  421.2 2.4 fusion.45
  423.8 1.2 copy-done.1
  425.0 1.4 slice_subtract_fusion.1
  426.4 1.2 pad_maximum_fusion
  (34 shorter events, 1.3 us)
Async XLA Ops:
  33.9 18.4 %collective-permute-start.1 = (bf16[2,96,1536]{2,0,1:T(2,128)(2,1)S(1)}, bf16[2,96,1536]{2,0,1:T(2,128)(2,1)S(1)}, u32[]{:S(2)}, u32[]{:S(2)}) collective-permute-start(bf16[2,96,1536]{2,0,1:T(2,128)(2,1)S(1)} %fusion.53), channel_id=1, source_target_pairs={{12,0},{0,4},{4,8},{8,12},{13,1},{1,5},{5,9},{9,13},{14,2},{2,6},{... | collective-permute-start | bytes 1769480 | tf_op jit(solution)/shard_map/ppermute | solution.py:35
  52.3 7.6 %collective-permute-start.2 = (bf16[2,96,1536]{2,0,1:T(2,128)(2,1)S(1)}, bf16[2,96,1536]{2,0,1:T(2,128)(2,1)S(1)}, u32[]{:S(2)}, u32[]{:S(2)}) collective-permute-start(bf16[2,96,1536]{2,0,1:T(2,128)(2,1)S(1)} %collective-permute-done.1), channel_id=1, source_target_pairs={{1,0},{2,1},{3,2},{0,3},{5,4},{6,5},{7,6},{4,7},{9,8},{10,9},{11,1... | collective-permute-start | bytes 1769480 | tf_op jit(solution)/shard_map/ppermute | solution.py:35
  61.3 28.7 %collective-permute-start.3 = (bf16[2,96,1536]{2,0,1:T(2,128)(2,1)S(1)}, bf16[2,96,1536]{2,0,1:T(2,128)(2,1)S(1)}, u32[]{:S(2)}, u32[]{:S(2)}) collective-permute-start(bf16[2,96,1536]{2,0,1:T(2,128)(2,1)S(1)} %broadcast_select_fusion.3), channel_id=1, source_target_pairs={{8,0},{12,4},{0,8},{4,12},{9,1},{13,5},{1,9},{5,13},{10,2},{14,6},... | collective-permute-start | bytes 1769480 | tf_op jit(solution)/shard_map/ppermute | solution.py:35
  90.0 44.3 %collective-permute-start.4 = (bf16[2,96,1536]{2,0,1:T(2,128)(2,1)S(1)}, bf16[2,96,1536]{2,0,1:T(2,128)(2,1)S(1)}, u32[]{:S(2)}, u32[]{:S(2)}) collective-permute-start(bf16[2,96,1536]{2,0,1:T(2,128)(2,1)S(1)} %collective-permute-done.3), channel_id=1, source_target_pairs={{2,0},{3,1},{0,2},{1,3},{6,4},{7,5},{4,6},{5,7},{10,8},{11,9},{8,1... | collective-permute-start | bytes 1769480 | tf_op jit(solution)/shard_map/ppermute | solution.py:35
  157.7 21.1 %collective-permute-start.5 = (bf16[2,1536,128]{2,1,0:T(8,128)(2,1)S(1)}, bf16[2,1536,128]{2,1,0:T(8,128)(2,1)S(1)}, u32[]{:S(2)}, u32[]{:S(2)}) collective-permute-start(bf16[2,1536,128]{2,1,0:T(8,128)(2,1)S(1)} %slice.100), channel_id=1, source_target_pairs={{12,0},{0,4},{4,8},{8,12},{13,1},{1,5},{5,9},{9,13},{14,2},{2,6},{... | collective-permute-start | bytes 2359304 | tf_op jit(solution)/shard_map/ppermute | solution.py:35
  178.9 9.5 %collective-permute-start.6 = (bf16[2,1536,128]{2,1,0:T(8,128)(2,1)S(1)}, bf16[2,1536,128]{2,1,0:T(8,128)(2,1)S(1)}, u32[]{:S(2)}, u32[]{:S(2)}) collective-permute-start(bf16[2,1536,128]{2,1,0:T(8,128)(2,1)S(1)} %collective-permute-done.5), channel_id=1, source_target_pairs={{1,0},{2,1},{3,2},{0,3},{5,4},{6,5},{7,6},{4,7},{9,8},{10,9},{11,1... | collective-permute-start | bytes 2359304 | tf_op jit(solution)/shard_map/ppermute | solution.py:35
  191.4 36.1 %collective-permute-start.7 = (bf16[2,1536,128]{2,1,0:T(8,128)(2,1)S(1)}, bf16[2,1536,128]{2,1,0:T(8,128)(2,1)S(1)}, u32[]{:S(2)}, u32[]{:S(2)}) collective-permute-start(bf16[2,1536,128]{2,1,0:T(8,128)(2,1)S(1)} %get-tuple-element.173), channel_id=1, source_target_pairs={{8,0},{12,4},{0,8},{4,12},{9,1},{13,5},{1,9},{5,13},{10,2},{14,6},... | collective-permute-start | bytes 2359304 | tf_op jit(solution)/shard_map/ppermute | solution.py:35
  227.5 19.6 %collective-permute-start.8 = (bf16[2,1536,128]{2,1,0:T(8,128)(2,1)S(1)}, bf16[2,1536,128]{2,1,0:T(8,128)(2,1)S(1)}, u32[]{:S(2)}, u32[]{:S(2)}) collective-permute-start(bf16[2,1536,128]{2,1,0:T(8,128)(2,1)S(1)} %collective-permute-done.7), channel_id=1, source_target_pairs={{2,0},{3,1},{0,2},{1,3},{6,4},{7,5},{4,6},{5,7},{10,8},{11,9},{8,1... | collective-permute-start | bytes 2359304 | tf_op jit(solution)/shard_map/ppermute | solution.py:35
  228.3 22.2 %copy-start.2 = (f32[2]{0:T(128)S(1)}, f32[2]{0:T(128)}, u32[]{:S(2)}) copy-start(f32[2]{0:T(128)} %param.9) | copy-start | bytes 28
  250.5 22.2 %collective-permute-start.9 = (bf16[2,1536,128]{2,1,0:T(8,128)(2,1)S(1)}, bf16[2,1536,128]{2,1,0:T(8,128)(2,1)S(1)}, u32[]{:S(2)}, u32[]{:S(2)}) collective-permute-start(bf16[2,1536,128]{2,1,0:T(8,128)(2,1)S(1)} %get-tuple-element.166), channel_id=1, source_target_pairs={{0,4},{4,8},{8,12},{12,0},{1,5},{5,9},{9,13},{13,1},{2,6},{6,10},{... | collective-permute-start | bytes 2359304 | tf_op jit(solution)/shard_map/ppermute | solution.py:20
  251.1 42.3 %collective-permute-start.10 = (bf16[2,1536,128]{2,1,0:T(8,128)(2,1)S(1)}, bf16[2,1536,128]{2,1,0:T(8,128)(2,1)S(1)}, u32[]{:S(2)}, u32[]{:S(2)}) collective-permute-start(bf16[2,1536,128]{2,1,0:T(8,128)(2,1)S(1)} %get-tuple-element.166), channel_id=1, source_target_pairs={{0,12},{4,0},{8,4},{12,8},{1,13},{5,1},{9,5},{13,9},{2,14},{6,2},{... | collective-permute-start | bytes 2359304 | tf_op jit(solution)/shard_map/ppermute | solution.py:25
  272.7 32.0 %collective-permute-start.11 = (bf16[2,1536,128]{2,1,0:T(8,128)(2,1)S(1)}, bf16[2,1536,128]{2,1,0:T(8,128)(2,1)S(1)}, u32[]{:S(2)}, u32[]{:S(2)}) collective-permute-start(bf16[2,1536,128]{2,1,0:T(8,128)(2,1)S(1)} %collective-permute-done.9), channel_id=1, source_target_pairs={{0,4},{4,8},{8,12},{12,0},{1,5},{5,9},{9,13},{13,1},{2,6},{6,10},{... | collective-permute-start | bytes 2359304 | tf_op jit(solution)/shard_map/ppermute | solution.py:20
  306.0 8.5 %copy-start = (bf16[2,1536,1536]{2,1,0:T(8,128)(2,1)S(1)}, bf16[2,1536,1536]{2,1,0:T(8,128)(2,1)}, u32[]{:S(2)}) copy-start(bf16[2,1536,1536]{2,1,0:T(8,128)(2,1)} %get-tuple-element.248) | copy-start | bytes 28311556 | tf_op jit(solution)/shard_map/while
  320.0 19.9 %collective-permute-start = (f32[2,1536,128]{1,2,0:T(8,128)S(1)}, f32[2,1536,128]{1,2,0:T(8,128)S(1)}, u32[]{:S(2)}, u32[]{:S(2)}) collective-permute-start(f32[2,1536,128]{1,2,0:T(8,128)S(1)} %maximum_add_fusion.3), channel_id=1, source_target_pairs={{3,0},{0,1},{1,2},{2,3},{7,4},{4,5},{5,6},{6,7},{11,8},{8,9},{9,10... | collective-permute-start | bytes 4718600 | tf_op jit(solution)/shard_map/while/body/eval_jaxpr/ppermute | solution.py:35
  339.9 8.5 %copy-start = (bf16[2,1536,1536]{2,1,0:T(8,128)(2,1)S(1)}, bf16[2,1536,1536]{2,1,0:T(8,128)(2,1)}, u32[]{:S(2)}) copy-start(bf16[2,1536,1536]{2,1,0:T(8,128)(2,1)} %get-tuple-element.248) | copy-start | bytes 28311556 | tf_op jit(solution)/shard_map/while
  353.9 19.9 %collective-permute-start = (f32[2,1536,128]{1,2,0:T(8,128)S(1)}, f32[2,1536,128]{1,2,0:T(8,128)S(1)}, u32[]{:S(2)}, u32[]{:S(2)}) collective-permute-start(f32[2,1536,128]{1,2,0:T(8,128)S(1)} %maximum_add_fusion.3), channel_id=1, source_target_pairs={{3,0},{0,1},{1,2},{2,3},{7,4},{4,5},{5,6},{6,7},{11,8},{8,9},{9,10... | collective-permute-start | bytes 4718600 | tf_op jit(solution)/shard_map/while/body/eval_jaxpr/ppermute | solution.py:35
  373.8 8.5 %copy-start = (bf16[2,1536,1536]{2,1,0:T(8,128)(2,1)S(1)}, bf16[2,1536,1536]{2,1,0:T(8,128)(2,1)}, u32[]{:S(2)}) copy-start(bf16[2,1536,1536]{2,1,0:T(8,128)(2,1)} %get-tuple-element.248) | copy-start | bytes 28311556 | tf_op jit(solution)/shard_map/while
  387.8 19.9 %collective-permute-start = (f32[2,1536,128]{1,2,0:T(8,128)S(1)}, f32[2,1536,128]{1,2,0:T(8,128)S(1)}, u32[]{:S(2)}, u32[]{:S(2)}) collective-permute-start(f32[2,1536,128]{1,2,0:T(8,128)S(1)} %maximum_add_fusion.3), channel_id=1, source_target_pairs={{3,0},{0,1},{1,2},{2,3},{7,4},{4,5},{5,6},{6,7},{11,8},{8,9},{9,10... | collective-permute-start | bytes 4718600 | tf_op jit(solution)/shard_map/while/body/eval_jaxpr/ppermute | solution.py:35
  408.2 10.5 %slice-start = ((s8[9437184]{0:T(1024)(128)(4,1)}), s8[4194304]{0:T(1024)(128)(4,1)S(1)}, s32[]{:S(2)}) async-start(s8[9437184]{0:T(1024)(128)(4,1)} %bitcast.106), calls=%async_computation | async-start | bytes 8388608
  408.2 10.5 %slice-start.1 = ((s8[9437184]{0:T(1024)(128)(4,1)}), s8[4194304]{0:T(1024)(128)(4,1)S(1)}, s32[]{:S(2)}) async-start(s8[9437184]{0:T(1024)(128)(4,1)} %bitcast.106), calls=%async_computation.1 | async-start | bytes 8388608
  413.5 5.3 %slice-start.2 = ((s8[9437184]{0:T(1024)(128)(4,1)}), s8[1048576]{0:T(1024)(128)(4,1)S(1)}, s32[]{:S(2)}) async-start(s8[9437184]{0:T(1024)(128)(4,1)} %bitcast.106), calls=%async_computation.2 | async-start | bytes 2097152
  423.6 1.4 copy-start.1
